TPU v7x, 256 devices: a whole 4x4x8 slice. The times are simulated.
256 devices in a mesh: pipe: 2 (over core), obs: 16 (over y, x), patch: 8 (over z).
Axes of the slice: x: 4, y: 4, z: 8, core: 2. Of those that a mesh axis runs over, the one named last changes fastest.
Arguments:
- patch_tokens: bfloat16 [4096, 2048], P('patch', 'obs'), may hold values from -40 to 40
- obs_tokens: bfloat16 [2048, 2048], P('patch', 'obs'), may hold values from -40 to 40
- footprint: int32 [32, 8], P('patch'), may hold values from 0 to 15, as said below
- list_counts: int32 [32], P('patch'), may hold values from 1 to 8
- footprint_bias: float32 [32, 8], P('patch'), may hold values from -4 to 290
- w_query: bfloat16 [2, 2048, 2048], P('pipe', None, 'obs'), may hold values from -0.125 to 0.125
- w_key: bfloat16 [2, 2048, 2048], P('pipe', None, 'obs'), may hold values from -0.125 to 0.125
- w_value: bfloat16 [2, 2048, 2048], P('pipe', None, 'obs'), may hold values from -0.125 to 0.125
- w_out: bfloat16 [2, 2048, 2048], P('pipe', 'obs'), may hold values from -0.125 to 0.125
- patch_gain: float32 [2, 2048], P('pipe'), may hold values from 0.1 to 1.9
- obs_gain: float32 [2, 2048], P('pipe'), may hold values from 0.1 to 1.9
Outputs:
- sections: bfloat16 [2, 4096, 2048], P('pipe', 'patch', 'obs')
Inputs may be any that keep to these rules, and one draw needn't show every extreme that they name: `footprint`: entries are global observation block indices. In each row the first list_counts entries (the live ones) are distinct, the rest are to be ignored. For a device along patch and any device along patch, all live entries of the first device's rows that lie in the second device's range of 2 blocks name one and the same block.
All inputs are finite; a program needn't handle non-finite values.
Results may differ from a plain program's by a relative error of at most 0.012.
Values may be sent and summed in bfloat16 or wider, within the bound.
No kernel may reach another device: no remote copies, remote signals or barrier semaphores. Data moves between devices by JAX's collectives and lax.ppermute only.
A program may use at most 64 MiB of HBM per device.

v0:
```python
import jax
import jax.numpy as jnp
from jax import lax
from jax.sharding import PartitionSpec as P

HS = 128
BLK = 128
MB = 128


def passed_along(value, axis, steps):
    count = lax.axis_size(axis)
    first, last = (max(0, -steps), min(count, count - steps))
    return lax.ppermute(value, axis, [(source, source + steps) for source in range(first, last)])


def rms_round(values, gain):
    widened = values.astype(jnp.float32)
    scaled = widened * lax.rsqrt(jnp.mean(widened * widened, axis=-1, keepdims=True) + 1e-05)
    return (scaled * gain).astype(jnp.bfloat16)


def store_rows(sections, out_piece, is_valid, row_start):
    current = lax.dynamic_slice_in_dim(sections, row_start, out_piece.shape[0], 1)
    kept = jnp.where(is_valid, out_piece[None], current)
    return lax.dynamic_update_slice_in_dim(sections, kept, row_start, 1)


def on_device(
    patch_tokens,
    obs_tokens,
    footprint,
    list_counts,
    footprint_bias,
    w_query,
    w_key,
    w_value,
    w_out,
    patch_gain,
    obs_gain,
):
    pipe_segment = lax.axis_index("pipe")
    segment_count = lax.axis_size("pipe")
    obs_column = lax.axis_index("obs")
    feature_part = patch_tokens.shape[1]
    full_features = feature_part * lax.axis_size("obs")
    head_width = w_query.shape[2]
    heads_here = head_width // HS
    list_slots = footprint.shape[1]
    micro_count = patch_tokens.shape[0] // MB
    blocks_micro = MB // BLK
    score_scale = HS ** (-0.5)
    observed = lax.all_gather(obs_tokens, "obs", axis=1, tiled=True)
    obs_normed = rms_round(observed, obs_gain[0])
    key_values = jnp.concatenate(
        [
            jnp.dot(obs_normed, w_key[0], preferred_element_type=jnp.float32).astype(jnp.bfloat16),
            jnp.dot(obs_normed, w_value[0], preferred_element_type=jnp.float32).astype(
                jnp.bfloat16
            ),
        ],
        axis=1,
    )
    local_blocks = key_values.reshape(-1, BLK, 2 * head_width)
    kv_table = lax.all_gather(local_blocks, "patch", axis=0, tiled=True)

    def attend_block(segment_input, micro_index):
        patch_normed = rms_round(segment_input, patch_gain[0])
        queries = (
            jnp.dot(patch_normed, w_query[0], preferred_element_type=jnp.float32) * score_scale
        ).astype(jnp.bfloat16)
        queries = queries.reshape(blocks_micro, BLK, heads_here, HS)
        first_block = micro_index * blocks_micro
        slot_part = lax.dynamic_slice_in_dim(footprint, first_block, blocks_micro, 0)
        count_part = lax.dynamic_slice_in_dim(list_counts, first_block, blocks_micro, 0)
        bias_part = lax.dynamic_slice_in_dim(footprint_bias, first_block, blocks_micro, 0)
        picked = kv_table[slot_part].reshape(blocks_micro, list_slots * BLK, 2 * head_width)
        key_part = picked[:, :, :head_width].reshape(blocks_micro, list_slots * BLK, heads_here, HS)
        value_part = picked[:, :, head_width:].reshape(
            blocks_micro, list_slots * BLK, heads_here, HS
        )
        scores = jnp.einsum(
            "bqhd,bkhd->bhqk", queries, key_part, preferred_element_type=jnp.float32
        )
        alive_mask = jnp.repeat(jnp.arange(list_slots)[None, :] < count_part[:, None], BLK, axis=1)
        added = jnp.repeat(bias_part, BLK, axis=1)
        scores = jnp.where(alive_mask[:, None, None, :], scores + added[:, None, None, :], -1e30)
        row_max = jnp.max(scores, axis=-1, keepdims=True)
        weights = jnp.exp(scores - row_max)
        weights = (weights / jnp.sum(weights, axis=-1, keepdims=True)).astype(jnp.bfloat16)
        context = jnp.einsum(
            "bhqk,bkhd->bqhd", weights, value_part, preferred_element_type=jnp.float32
        ).astype(jnp.bfloat16)
        context = context.reshape(MB, head_width)
        return jnp.dot(context, w_out[0], preferred_element_type=jnp.float32)

    def spare_block(segment_input, micro_index):
        return jnp.zeros((MB, full_features), jnp.float32)

    tick_total = micro_count + segment_count - 1
    sections = jnp.zeros((1, patch_tokens.shape[0], feature_part), jnp.bfloat16)
    rows_all = lax.all_gather(patch_tokens, "obs", axis=1, tiled=True)
    arriving = jnp.zeros((MB, full_features), jnp.bfloat16)
    for tick_num in range(tick_total):
        tick_micro = tick_num - pipe_segment
        is_valid = (tick_micro >= 0) & (tick_micro < micro_count)
        micro_index = jnp.clip(tick_micro, 0, micro_count - 1)
        own_rows = lax.dynamic_slice_in_dim(rows_all, micro_index * MB, MB, 0)
        segment_input = jnp.where(pipe_segment == 0, own_rows, arriving)
        partial_value = lax.cond(is_valid, attend_block, spare_block, segment_input, micro_index)
        head_total = lax.psum(partial_value.astype(jnp.bfloat16), "obs").astype(jnp.float32)
        segment_output = (segment_input.astype(jnp.float32) + head_total).astype(jnp.bfloat16)
        out_piece = lax.dynamic_slice_in_dim(
            segment_output, obs_column * feature_part, feature_part, 1
        )
        sections = store_rows(sections, out_piece, is_valid, micro_index * MB)
        if tick_num + 1 < tick_total:
            arriving = passed_along(segment_output, "pipe", 1)
    return sections


def solution(mesh):
    in_specs = (
        P("patch", "obs"),
        P("patch", "obs"),
        P("patch", None),
        P("patch"),
        P("patch", None),
        P("pipe", None, "obs"),
        P("pipe", None, "obs"),
        P("pipe", None, "obs"),
        P("pipe", "obs", None),
        P("pipe", None),
        P("pipe", None),
    )
    out_specs = P("pipe", "patch", "obs")
    return jax.shard_map(
        on_device, mesh=mesh, in_specs=in_specs, out_specs=out_specs, check_vma=False
    )
```

profile of v0, /device:TPU:2, one launch (start us, length us, event | category | flops | bytes accessed | tf_op | source)
XLA Modules:
  0.0 700.2 jit_solution(2485516238832570236)
XLA Ops:
  6.5 0.7 all-gather.6.cloned.1.call-update
  7.3 0.7 all-gather.4.cloned.1.call-update
  8.1 52.5 %all-gather.6.cloned.1.call-done = bf16[256,2048]{1,0:T(8,128)(2,1)} async-done(((bf16[256,128]{1,0:T(8,128)(2,1)}), bf16[256,2048]{1,0:T(8,128)(2,1)}) %all-gather.6.cloned.1.call-update) | async-done | bytes 1048592 | tf_op jit(solution)/shard_map/all_gather | solution.py:53
  60.6 1.6 fusion.120
  62.2 1.8 convolution_convert_fusion.5
  64.7 0.8 copy.14
  65.5 48.9 %all-gather.4.cloned.1.call-done = bf16[512,2048]{1,0:T(8,128)(2,1)} async-done(((bf16[512,128]{1,0:T(8,128)(2,1)}), bf16[512,2048]{1,0:T(8,128)(2,1)}) %all-gather.4.cloned.1.call-update) | async-done | bytes 2097168 | tf_op jit(solution)/shard_map/all_gather | solution.py:102
  114.4 1.1 dynamic-slice_select_fusion.4
  115.6 38.8 %all-gather.8.cloned.1.call-done = bf16[16,128,256]{2,1,0:T(8,128)(2,1)} async-done(((bf16[2,128,256]{2,1,0:T(8,128)(2,1)}), bf16[16,128,256]{2,1,0:T(8,128)(2,1)}) %all-gather.8.cloned.1.call-update) | async-done | bytes 1048592 | tf_op jit(solution)/shard_map/all_gather | solution.py:65
  154.4 6.1 conditional.5
  154.5 1.8 gather_fusion
  156.5 0.6 dynamic_slice.36
  157.1 0.6 iota_compare_fusion
  157.9 0.6 fusion.133
  158.7 1.8 fusion.3
  160.5 0.8 copy-done.2
  161.4 93.9 %all-reduce.6.cloned.1.call-done = bf16[128,2048]{1,0:T(8,128)(2,1)} async-done(((bf16[128,2048]{1,0:T(8,128)(2,1)}), bf16[128,2048]{1,0:T(8,128)(2,1)}) %all-reduce.6.cloned.1.call-update) | async-done | bytes 524304 | tf_op jit(solution)/shard_map/psum | solution.py:111
  255.3 2.1 add_convert_fusion.3
  257.5 1.3 collective-permute-start
  258.8 1.7 collective-permute-done
  260.5 1.2 dynamic-slice_select_fusion.3
  261.7 6.7 conditional.6
  261.7 0.8 copy-done.15
  262.5 0.6 gather_fusion.1
  263.3 0.6 dynamic_slice.70
  263.9 0.6 iota_compare_fusion.1
  264.6 1.6 fusion.138
  266.5 1.9 fusion.27
  268.4 0.8 copy-done.3
  269.3 95.4 %all-reduce.8.cloned.1.call-done = bf16[128,2048]{1,0:T(8,128)(2,1)} async-done(((bf16[128,2048]{1,0:T(8,128)(2,1)}), bf16[128,2048]{1,0:T(8,128)(2,1)}) %all-reduce.8.cloned.1.call-update) | async-done | bytes 524304 | tf_op jit(solution)/shard_map/psum | solution.py:111
  364.6 1.2 add_convert_fusion.2
  365.8 1.3 collective-permute-start.1
  367.1 1.5 collective-permute-done.1
  368.6 1.2 dynamic-slice_select_fusion.2
  369.8 7.7 %conditional.7 = (bf16[128,2048]{1,0:T(8,128)(2,1)S(1)}) conditional(s32[]{:T(128)} %convert_element_type.212, () %tuple.39, (s32[]{:T(128)}, s32[4,8]{1,0:T(4,128)S(1)}, bf16[16,128,256]{2,1,0:T(8,128)(2,1)S(1)}, s32[4]{0:T(128)S(1)}, bf16[128,2048]{1,0:T(8,128)(2,1)S(1)}, /*index=5*/f32[1,2048]{1,0:T(1,128)S(1)}, ...), branch_computations={%region_13.14_spmd, %region_14.18_spmd} | conditional | flops 204260256 | bytes 7891790 | solution.py:110
  369.9 1.4 gather_fusion.2
  371.5 0.6 dynamic_slice.74
  372.7 1.7 fusion.143
  374.4 0.8 copy-done.10
  375.4 2.0 fusion.51
  377.5 0.8 copy-done.4
  378.4 95.4 %all-reduce.10.cloned.1.call-done = bf16[128,2048]{1,0:T(8,128)(2,1)} async-done(((bf16[128,2048]{1,0:T(8,128)(2,1)}), bf16[128,2048]{1,0:T(8,128)(2,1)}) %all-reduce.10.cloned.1.call-update) | async-done | bytes 524304 | tf_op jit(solution)/shard_map/psum | solution.py:111
  473.7 1.2 add_convert_fusion.1
  474.9 2.1 collective-permute-start.2
  477.0 0.8 collective-permute-done.2
  477.9 1.2 dynamic-slice_select_fusion.1
  479.1 7.8 %conditional.8 = (bf16[128,2048]{1,0:T(8,128)(2,1)S(1)}) conditional(s32[]{:T(128)} %convert_element_type.217, () %tuple.41, (s32[]{:T(128)}, s32[4,8]{1,0:T(4,128)S(1)}, bf16[16,128,256]{2,1,0:T(8,128)(2,1)S(1)}, s32[4]{0:T(128)S(1)}, bf16[128,2048]{1,0:T(8,128)(2,1)S(1)}, /*index=5*/f32[1,2048]{1,0:T(1,128)S(1)}, ...), branch_computations={%region_19.20_spmd, %region_20.24_spmd} | conditional | flops 204260256 | bytes 7891790 | solution.py:110
  479.2 1.4 gather_fusion.3
  480.8 0.7 dynamic_slice.78
  481.4 0.6 iota_compare_fusion.3
  482.1 1.7 fusion.148
  483.9 0.8 copy-done.11
  484.9 2.0 fusion.75
  486.9 0.8 copy-done.5
  487.8 95.6 %all-reduce.12.cloned.1.call-done = bf16[128,2048]{1,0:T(8,128)(2,1)} async-done(((bf16[128,2048]{1,0:T(8,128)(2,1)}), bf16[128,2048]{1,0:T(8,128)(2,1)}) %all-reduce.12.cloned.1.call-update) | async-done | bytes 524304 | tf_op jit(solution)/shard_map/psum | solution.py:111
  583.3 1.2 add_convert_fusion
  584.5 2.1 collective-permute-start.3
  586.6 0.8 collective-permute-done.3
  587.5 1.2 dynamic-slice_select_fusion
  588.7 0.8 copy-done.6
  589.5 0.8 bitcast_dynamic-update-slice_fusion
  590.4 0.8 fusion.131
  591.2 100.7 %all-reduce.14.cloned.1.call-done = bf16[128,2048]{1,0:T(8,128)(2,1)} async-done(((bf16[128,2048]{1,0:T(8,128)(2,1)}), bf16[128,2048]{1,0:T(8,128)(2,1)}) %all-reduce.14.cloned.1.call-update) | async-done | bytes 524304 | tf_op jit(solution)/shard_map/psum | solution.py:111
  691.9 1.4 fusion.129
  (89 shorter events, 4.2 us)
Async XLA Ops:
  6.5 55.6 %copy-start = (bf16[1,2048,128]{2,1,0:T(8,128)(2,1)S(1)}, bf16[1,2048,128]{2,1,0:T(8,128)(2,1)}, u32[]{:S(2)}) copy-start(bf16[1,2048,128]{2,1,0:T(8,128)(2,1)} %param.28) | copy-start | bytes 1572868
  6.5 57.4 %copy-start.16 = (f32[1,2048]{1,0:T(1,128)S(1)}, f32[1,2048]{1,0:T(1,128)}, u32[]{:S(2)}) copy-start(f32[1,2048]{1,0:T(1,128)} %param.31) | copy-start | bytes 24580
  6.5 57.4 %copy-start.13 = (bf16[1,2048,128]{2,1,0:T(8,128)(2,1)S(1)}, bf16[1,2048,128]{2,1,0:T(8,128)(2,1)}, u32[]{:S(2)}) copy-start(bf16[1,2048,128]{2,1,0:T(8,128)(2,1)} %param.27) | copy-start | bytes 1572868
  6.5 54.0 %all-gather.6.cloned.1.call-start = ((), (), s32[]{:S(2)}) async-start(), calls=%async_computation.1 | async-start | bytes 1114112 | tf_op jit(solution)/shard_map/all_gather | solution.py:53
  7.3 107.2 %all-gather.4.cloned.1.call-start = ((), (), s32[]{:S(2)}) async-start(), calls=%async_computation | async-start | bytes 2228224 | tf_op jit(solution)/shard_map/all_gather | solution.py:102
  8.0 146.4 %all-gather.8.cloned.1.call-start = ((), (), s32[]{:S(2)}) async-start(), calls=%async_computation.2 | async-start | bytes 1179648 | tf_op jit(solution)/shard_map/all_gather | solution.py:65
  60.5 3.4 copy-start.7
  64.0 90.4 %copy-start.14 = (bf16[1,2048,128]{2,1,0:T(8,128)(2,1)S(1)}, bf16[1,2048,128]{2,1,0:T(8,128)(2,1)}, u32[]{:S(2)}) copy-start(bf16[1,2048,128]{2,1,0:T(8,128)(2,1)} %param.26) | copy-start | bytes 1572868
  64.0 90.4 %copy-start.17 = (f32[1,2048]{1,0:T(1,128)S(1)}, f32[1,2048]{1,0:T(1,128)}, u32[]{:S(2)}) copy-start(f32[1,2048]{1,0:T(1,128)} %param.30) | copy-start | bytes 24580
  64.0 90.4 %copy-start.18 = (s32[4,8]{1,0:T(4,128)S(1)}, s32[4,8]{1,0:T(4,128)}, u32[]{:S(2)}) copy-start(s32[4,8]{1,0:T(4,128)} %param.23) | copy-start | bytes 388
  64.0 90.4 %copy-start.19 = (f32[4,8]{1,0:T(4,128)S(1)}, f32[4,8]{1,0:T(4,128)}, u32[]{:S(2)}) copy-start(f32[4,8]{1,0:T(4,128)} %param.25) | copy-start | bytes 388
  64.0 90.3 %copy-start.20 = (s32[4]{0:T(128)S(1)}, s32[4]{0:T(128)}, u32[]{:S(2)}) copy-start(s32[4]{0:T(128)} %param.24) | copy-start | bytes 52
  65.4 189.9 %all-reduce.6.cloned.1.call-start = ((), (), s32[]{:S(2)}) async-start(), calls=%async_computation.3 | async-start | bytes 1048576 | tf_op jit(solution)/shard_map/psum | solution.py:111
  160.5 0.8 copy-start.2
  160.5 101.1 %copy-start.1 = (bf16[16,128,256]{2,1,0:T(8,128)(2,1)S(1)}, bf16[16,128,256]{2,1,0:T(8,128)(2,1)}, u32[]{:S(2)}) copy-start(bf16[16,128,256]{2,1,0:T(8,128)(2,1)} %all-gather.8.cloned.1.call-done) | copy-start | bytes 3145732
  161.3 203.3 %all-reduce.8.cloned.1.call-start = ((), (), s32[]{:S(2)}) async-start(), calls=%async_computation.4 | async-start | bytes 1048576 | tf_op jit(solution)/shard_map/psum | solution.py:111
  257.5 3.0 collective-permute-start
  261.7 0.8 copy-start.15
  263.1 3.1 copy-start.12
  268.4 0.8 copy-start.3
  269.2 204.5 %all-reduce.10.cloned.1.call-start = ((), (), s32[]{:S(2)}) async-start(), calls=%async_computation.5 | async-start | bytes 1048576 | tf_op jit(solution)/shard_map/psum | solution.py:111
  365.8 2.8 collective-permute-start.1
  374.4 0.8 copy-start.10
  377.5 0.8 copy-start.4
  378.3 205.0 %all-reduce.12.cloned.1.call-start = ((), (), s32[]{:S(2)}) async-start(), calls=%async_computation.6 | async-start | bytes 1048576 | tf_op jit(solution)/shard_map/psum | solution.py:111
  474.9 4.1 copy-start.8
  474.9 2.9 collective-permute-start.2
  483.8 0.8 copy-start.11
  486.9 0.8 copy-start.5
  487.7 204.2 %all-reduce.14.cloned.1.call-start = ((), (), s32[]{:S(2)}) async-start(), calls=%async_computation.7 | async-start | bytes 1048576 | tf_op jit(solution)/shard_map/psum | solution.py:111
  584.5 2.9 collective-permute-start.3
  588.7 0.8 copy-start.6
  591.2 100.7 %copy-start.9 = (bf16[1,512,128]{2,1,0:T(8,128)(2,1)}, bf16[1,512,128]{2,1,0:T(8,128)(2,1)S(1)}, u32[]{:S(2)}) copy-start(bf16[1,512,128]{2,1,0:T(8,128)(2,1)S(1)} %fusion.130) | copy-start | bytes 393220
Sparse Core Ops, SparseCore 0:
  9.7 50.7 all-gather.5
  63.0 51.4 all-gather.3
  116.2 38.1 all-gather.7
  161.4 93.8 all-reduce.5
  269.3 95.2 all-reduce.7
  378.4 95.2 all-reduce.9
  487.9 95.4 all-reduce.11
  589.6 102.2 all-reduce.13
where the time goes:
time: 701 us; the launch traced here: 700 us
  waiting for transfers between devices  628 us (90%)
  other arithmetic  20.3 us (3%)
  matrix products  15.8 us (2%)
  local copies, waits for them, and re-layouts  15.4 us (2%)
  between operations  13.8 us (2%)
  starting transfers between devices  7.12 us (1%)
    psum x5, waiting for transfers between devices, on_device(): lax.psum(partial_value.astype(jnp.bfloat16), 'obs').astype(jnp.float32)  481 us
    all_gather x1, waiting for transfers between devices, on_device(): observed = lax.all_gather(obs_tokens, 'obs', axis=1, tiled=True)  52.5 us
    all_gather x1, waiting for transfers between devices, on_device(): rows_all = lax.all_gather(patch_tokens, 'obs', axis=1, tiled=True)  48.9 us
    all_gather x1, waiting for transfers between devices, on_device(): kv_table = lax.all_gather(local_blocks, 'patch', axis=0, tiled=True)  38.8 us
  transfers between devices with their start and end apart: 12, of which 12 were waited for; matrix products, arithmetic and copies ran while one was open for 1% of the time, Pallas kernels for 0%

commit v1 on v0

--- a/solution.py
+++ b/solution.py
@@ -62,7 +62,9 @@
         axis=1,
     )
     local_blocks = key_values.reshape(-1, BLK, 2 * head_width)
-    kv_table = lax.all_gather(local_blocks, "patch", axis=0, tiled=True)
+    kv_table = jnp.concatenate(
+        lax.all_to_all(jnp.stack([local_blocks] * lax.axis_size("patch")), "patch", 0, 0), axis=0
+    )
 
     def attend_block(segment_input, micro_index):
         patch_normed = rms_round(segment_input, patch_gain[0])

time: 701 us -> 662 us (0.944)
  waiting for transfers between devices: 628 us -> 582 us
    all_gather x1 -> x0, waiting for transfers between devices: 38.8 us -> none  [on_device(): kv_table = lax.all_gather(local_blocks, 'patch', axis=0, tiled=True)]
    all_gather x1, waiting for transfers between devices: 48.9 us -> 41.5 us  [on_device(): rows_all = lax.all_gather(patch_tokens, 'obs', axis=1, tiled=True)]
    all_to_all x0 -> x1, starting transfers between devices: none -> 7.02 us  [on_device(): lax.all_to_all(jnp.stack([local_blocks] * lax.axis_size('patch')), 'patch...]
  transfers between devices with their start and end apart: 12 -> 12, of which waited for: 12 -> 11; matrix products, arithmetic and copies ran while one was open for 1% -> 1% of each run, Pallas kernels for 0% -> 0%
where the time goes in v1:
time: 662 us; the launch traced here: 661 us
  waiting for transfers between devices  582 us (88%)
  other arithmetic  20.2 us (3%)
  matrix products  16.8 us (3%)
  starting transfers between devices  14.1 us (2%)
  between operations  13.8 us (2%)
  local copies, waits for them, and re-layouts  13.7 us (2%)
    psum x5, waiting for transfers between devices, on_device(): lax.psum(partial_value.astype(jnp.bfloat16), 'obs').astype(jnp.float32)  482 us
    all_gather x1, waiting for transfers between devices, on_device(): observed = lax.all_gather(obs_tokens, 'obs', axis=1, tiled=True)  52.5 us
    all_gather x1, waiting for transfers between devices, on_device(): rows_all = lax.all_gather(patch_tokens, 'obs', axis=1, tiled=True)  41.5 us
  transfers between devices with their start and end apart: 12, of which 11 were waited for; matrix products, arithmetic and copies ran while one was open for 1% of the time, Pallas kernels for 0%

profile of v1, /device:TPU:2, one launch (start us, length us, event | category | flops | bytes accessed | tf_op | source)
XLA Modules:
  0.0 661.2 jit_solution(1966888730843323600)
XLA Ops:
  6.5 0.7 all-gather.5.cloned.1.call-update
  7.3 0.7 all-gather.3.cloned.1.call-update
  8.0 52.5 %all-gather.5.cloned.1.call-done = bf16[256,2048]{1,0:T(8,128)(2,1)} async-done(((bf16[256,128]{1,0:T(8,128)(2,1)}), bf16[256,2048]{1,0:T(8,128)(2,1)}) %all-gather.5.cloned.1.call-update) | async-done | bytes 1048592 | tf_op jit(solution)/shard_map/all_gather | solution.py:53
  60.6 1.6 fusion.120
  62.2 1.8 convolution_convert_fusion.5
  64.0 0.6 convolution_convert_fusion.6
  64.7 1.1 stack.3
  65.8 7.0 %all-to-all-start = ((bf16[8,2,128,256]{3,2,1,0:T(8,128)(2,1)}), bf16[8,2,128,256]{3,2,1,0:T(8,128)(2,1)S(1)}, u32[]{:S(2)}, u32[]{:S(2)}) async-start(bf16[8,2,128,256]{3,2,1,0:T(8,128)(2,1)} %stack.3), calls=%async_computation | async-start | bytes 2097152 | tf_op jit(solution)/shard_map/all_to_all | solution.py:66
  72.9 41.5 %all-gather.3.cloned.1.call-done = bf16[512,2048]{1,0:T(8,128)(2,1)} async-done(((bf16[512,128]{1,0:T(8,128)(2,1)}), bf16[512,2048]{1,0:T(8,128)(2,1)}) %all-gather.3.cloned.1.call-update) | async-done | bytes 2097168 | tf_op jit(solution)/shard_map/all_gather | solution.py:104
  114.4 1.1 dynamic-slice_select_fusion.4
  115.6 5.9 conditional.5
  115.7 0.6 gather_fusion
  116.5 0.6 dynamic_slice.36
  117.1 0.6 iota_compare_fusion
  117.8 1.6 fusion.133
  119.7 1.8 fusion.3
  121.5 0.8 copy-done.1
  122.4 95.2 %all-reduce.6.cloned.1.call-done = bf16[128,2048]{1,0:T(8,128)(2,1)} async-done(((bf16[128,2048]{1,0:T(8,128)(2,1)}), bf16[128,2048]{1,0:T(8,128)(2,1)}) %all-reduce.6.cloned.1.call-update) | async-done | bytes 524304 | tf_op jit(solution)/shard_map/psum | solution.py:113
  217.6 2.2 add_convert_fusion.3
  219.8 1.3 collective-permute-start
  221.1 1.7 collective-permute-done
  222.8 1.2 dynamic-slice_select_fusion.3
  224.0 6.0 conditional.6
  224.1 0.6 gather_fusion.1
  224.9 0.6 dynamic_slice.70
  225.5 0.6 iota_compare_fusion.1
  226.2 1.6 fusion.138
  228.0 1.9 fusion.27
  229.9 0.8 copy-done.2
  230.8 95.3 %all-reduce.8.cloned.1.call-done = bf16[128,2048]{1,0:T(8,128)(2,1)} async-done(((bf16[128,2048]{1,0:T(8,128)(2,1)}), bf16[128,2048]{1,0:T(8,128)(2,1)}) %all-reduce.8.cloned.1.call-update) | async-done | bytes 524304 | tf_op jit(solution)/shard_map/psum | solution.py:113
  326.1 1.2 add_convert_fusion.2
  327.3 1.3 collective-permute-start.1
  328.6 1.5 collective-permute-done.1
  330.1 1.2 dynamic-slice_select_fusion.2
  331.3 7.7 %conditional.7 = (bf16[128,2048]{1,0:T(8,128)(2,1)S(1)}) conditional(s32[]{:T(128)} %convert_element_type.212, () %tuple.39, (s32[]{:T(128)}, s32[4,8]{1,0:T(4,128)S(1)}, bf16[16,128,256]{2,1,0:T(8,128)(2,1)S(1)}, s32[4]{0:T(128)S(1)}, bf16[128,2048]{1,0:T(8,128)(2,1)S(1)}, /*index=5*/f32[1,2048]{1,0:T(1,128)S(1)}, ...), branch_computations={%region_13.14_spmd, %region_14.18_spmd} | conditional | flops 204260256 | bytes 7891790 | solution.py:112
  331.4 1.4 gather_fusion.2
  333.0 0.6 dynamic_slice.74
  334.1 1.7 fusion.143
  335.9 0.8 copy-done.9
  336.9 2.0 fusion.51
  338.9 0.8 copy-done.3
  339.8 95.3 %all-reduce.10.cloned.1.call-done = bf16[128,2048]{1,0:T(8,128)(2,1)} async-done(((bf16[128,2048]{1,0:T(8,128)(2,1)}), bf16[128,2048]{1,0:T(8,128)(2,1)}) %all-reduce.10.cloned.1.call-update) | async-done | bytes 524304 | tf_op jit(solution)/shard_map/psum | solution.py:113
  435.1 1.2 add_convert_fusion.1
  436.3 2.1 collective-permute-start.2
  438.4 0.9 collective-permute-done.2
  439.2 1.2 dynamic-slice_select_fusion.1
  440.4 7.7 %conditional.8 = (bf16[128,2048]{1,0:T(8,128)(2,1)S(1)}) conditional(s32[]{:T(128)} %convert_element_type.217, () %tuple.41, (s32[]{:T(128)}, s32[4,8]{1,0:T(4,128)S(1)}, bf16[16,128,256]{2,1,0:T(8,128)(2,1)S(1)}, s32[4]{0:T(128)S(1)}, bf16[128,2048]{1,0:T(8,128)(2,1)S(1)}, /*index=5*/f32[1,2048]{1,0:T(1,128)S(1)}, ...), branch_computations={%region_19.20_spmd, %region_20.24_spmd} | conditional | flops 204260256 | bytes 7891790 | solution.py:112
  440.5 1.4 gather_fusion.3
  442.1 0.6 dynamic_slice.78
  442.7 0.6 iota_compare_fusion.3
  443.3 1.7 fusion.148
  445.0 0.8 copy-done.10
  446.1 2.0 fusion.75
  448.1 0.8 copy-done.4
  449.0 95.5 %all-reduce.12.cloned.1.call-done = bf16[128,2048]{1,0:T(8,128)(2,1)} async-done(((bf16[128,2048]{1,0:T(8,128)(2,1)}), bf16[128,2048]{1,0:T(8,128)(2,1)}) %all-reduce.12.cloned.1.call-update) | async-done | bytes 524304 | tf_op jit(solution)/shard_map/psum | solution.py:113
  544.5 1.2 add_convert_fusion
  545.7 2.1 collective-permute-start.3
  547.8 0.9 collective-permute-done.3
  548.6 1.2 dynamic-slice_select_fusion
  549.9 0.8 copy-done.5
  550.7 0.8 bitcast_dynamic-update-slice_fusion
  551.6 0.8 fusion.131
  552.4 100.5 %all-reduce.14.cloned.1.call-done = bf16[128,2048]{1,0:T(8,128)(2,1)} async-done(((bf16[128,2048]{1,0:T(8,128)(2,1)}), bf16[128,2048]{1,0:T(8,128)(2,1)}) %all-reduce.14.cloned.1.call-update) | async-done | bytes 524304 | tf_op jit(solution)/shard_map/psum | solution.py:113
  652.9 1.4 fusion.129
  (83 shorter events, 3.6 us)
Async XLA Ops:
  6.5 55.6 %copy-start = (bf16[1,2048,128]{2,1,0:T(8,128)(2,1)S(1)}, bf16[1,2048,128]{2,1,0:T(8,128)(2,1)}, u32[]{:S(2)}) copy-start(bf16[1,2048,128]{2,1,0:T(8,128)(2,1)} %param.28) | copy-start | bytes 1572868
  6.5 57.4 %copy-start.13 = (f32[1,2048]{1,0:T(1,128)S(1)}, f32[1,2048]{1,0:T(1,128)}, u32[]{:S(2)}) copy-start(f32[1,2048]{1,0:T(1,128)} %param.31) | copy-start | bytes 24580
  6.5 57.4 %copy-start.12 = (bf16[1,2048,128]{2,1,0:T(8,128)(2,1)S(1)}, bf16[1,2048,128]{2,1,0:T(8,128)(2,1)}, u32[]{:S(2)}) copy-start(bf16[1,2048,128]{2,1,0:T(8,128)(2,1)} %param.27) | copy-start | bytes 1572868
  6.5 54.0 %all-gather.5.cloned.1.call-start = ((), (), s32[]{:S(2)}) async-start(), calls=%async_computation.2 | async-start | bytes 1114112 | tf_op jit(solution)/shard_map/all_gather | solution.py:53
  7.3 107.2 %all-gather.3.cloned.1.call-start = ((), (), s32[]{:S(2)}) async-start(), calls=%async_computation.1 | async-start | bytes 2228224 | tf_op jit(solution)/shard_map/all_gather | solution.py:104
  60.5 3.4 copy-start.6
  64.7 50.9 %copy-start.14 = (f32[1,2048]{1,0:T(1,128)S(1)}, f32[1,2048]{1,0:T(1,128)}, u32[]{:S(2)}) copy-start(f32[1,2048]{1,0:T(1,128)} %param.30) | copy-start | bytes 24580
  64.7 50.9 %copy-start.15 = (s32[4,8]{1,0:T(4,128)S(1)}, s32[4,8]{1,0:T(4,128)}, u32[]{:S(2)}) copy-start(s32[4,8]{1,0:T(4,128)} %param.23) | copy-start | bytes 388
  64.7 50.9 %copy-start.16 = (f32[4,8]{1,0:T(4,128)S(1)}, f32[4,8]{1,0:T(4,128)}, u32[]{:S(2)}) copy-start(f32[4,8]{1,0:T(4,128)} %param.25) | copy-start | bytes 388
  64.7 50.9 %copy-start.17 = (s32[4]{0:T(128)S(1)}, s32[4]{0:T(128)}, u32[]{:S(2)}) copy-start(s32[4]{0:T(128)} %param.24) | copy-start | bytes 52
  65.8 49.7 %all-to-all-start = ((bf16[8,2,128,256]{3,2,1,0:T(8,128)(2,1)}), bf16[8,2,128,256]{3,2,1,0:T(8,128)(2,1)S(1)}, u32[]{:S(2)}, u32[]{:S(2)}) async-start(bf16[8,2,128,256]{3,2,1,0:T(8,128)(2,1)} %stack.3), calls=%async_computation | async-start | bytes 2097152 | tf_op jit(solution)/shard_map/all_to_all | solution.py:66
  72.9 144.8 %all-reduce.6.cloned.1.call-start = ((), (), s32[]{:S(2)}) async-start(), calls=%async_computation.3 | async-start | bytes 1048576 | tf_op jit(solution)/shard_map/psum | solution.py:113
  121.5 0.8 copy-start.1
  122.3 203.8 %all-reduce.8.cloned.1.call-start = ((), (), s32[]{:S(2)}) async-start(), calls=%async_computation.4 | async-start | bytes 1048576 | tf_op jit(solution)/shard_map/psum | solution.py:113
  219.8 3.0 collective-permute-start
  224.7 3.2 copy-start.11
  229.9 0.8 copy-start.2
  230.7 204.3 %all-reduce.10.cloned.1.call-start = ((), (), s32[]{:S(2)}) async-start(), calls=%async_computation.5 | async-start | bytes 1048576 | tf_op jit(solution)/shard_map/psum | solution.py:113
  327.3 2.8 collective-permute-start.1
  335.8 0.8 copy-start.9
  338.9 0.8 copy-start.3
  339.7 204.8 %all-reduce.12.cloned.1.call-start = ((), (), s32[]{:S(2)}) async-start(), calls=%async_computation.6 | async-start | bytes 1048576 | tf_op jit(solution)/shard_map/psum | solution.py:113
  436.3 4.1 copy-start.7
  436.3 2.9 collective-permute-start.2
  445.0 0.8 copy-start.10
  448.1 0.8 copy-start.4
  448.9 204.0 %all-reduce.14.cloned.1.call-start = ((), (), s32[]{:S(2)}) async-start(), calls=%async_computation.7 | async-start | bytes 1048576 | tf_op jit(solution)/shard_map/psum | solution.py:113
  545.7 2.9 collective-permute-start.3
  549.9 0.8 copy-start.5
  552.4 100.5 %copy-start.8 = (bf16[1,512,128]{2,1,0:T(8,128)(2,1)}, bf16[1,512,128]{2,1,0:T(8,128)(2,1)S(1)}, u32[]{:S(2)}) copy-start(bf16[1,512,128]{2,1,0:T(8,128)(2,1)S(1)} %fusion.130) | copy-start | bytes 393220
Sparse Core Ops, SparseCore 0:
  9.7 50.7 all-gather.4
  63.0 51.4 all-gather.2
  122.4 95.1 all-reduce.5
  230.9 95.1 all-reduce.7
  339.8 95.1 all-reduce.9
  449.1 95.4 all-reduce.11
  550.8 102.0 all-reduce.13
